TPU v7x, 512 devices: a whole 4x4x16 slice. The times are simulated.
512 devices in a mesh: section: 4 (over x), dp: 16 (over z), expert: 8 (over y, core).
Axes of the slice: x: 4, y: 4, z: 16, core: 2. Of those that a mesh axis runs over, the one named last changes fastest.
Arguments:
- section_input: bfloat16 [4, 16384, 1024], P('section', ('dp', 'expert')), may hold values from -6 to 6
- saved_input: bfloat16 [4, 16384, 1024], P('section', ('dp', 'expert')), may hold values from -6 to 6
- cotangent: bfloat16 [4, 16384, 1024], P('section', ('dp', 'expert')), may hold values from -6 to 6
- routes_forward: int32 [4, 16384, 8], P('section', ('dp', 'expert')), may hold values from 0 to 63, as said below
- gates_forward: float32 [4, 16384, 8], P('section', ('dp', 'expert')), may hold values from 0.5 to 2
- routes_backward: int32 [4, 16384, 8], P('section', ('dp', 'expert')), may hold values from 0 to 63, as said below
- gates_backward: float32 [4, 16384, 8], P('section', ('dp', 'expert')), may hold values from 0.5 to 2
- gate_weight: bfloat16 [4, 8, 1024, 512], P('section', 'expert', 'dp'), may hold values from -0.1875 to 0.1875
- up_weight: bfloat16 [4, 8, 1024, 512], P('section', 'expert', 'dp'), may hold values from -0.1875 to 0.1875
- down_weight: bfloat16 [4, 8, 512, 1024], P('section', 'expert', 'dp'), may hold values from -0.25 to 0.25
Outputs:
- handed: bfloat16 [4, 16384, 1024], P('section', ('dp', 'expert'))
- grad_back: bfloat16 [4, 16384, 1024], P('section', ('dp', 'expert'))
- grad_gate: float32 [4, 8, 1024, 512], P('section', 'expert', 'dp')
- grad_up: float32 [4, 8, 1024, 512], P('section', 'expert', 'dp')
- grad_down: float32 [4, 8, 512, 1024], P('section', 'expert', 'dp')
Inputs may be any that keep to these rules, and one draw needn't show every extreme that they name: `routes_forward`: each token names 8 different experts. In every layer, every block of 128 tokens of one device names each expert below 8 between 1 and 32 times, and in every layer some expert below 8 is named exactly 32 times by every block. `routes_backward`: as routes_forward.
All inputs are finite; a program needn't handle non-finite values.
Results may differ from a plain program's by a relative error of at most 0.017.
Values may be sent and summed in bfloat16 or wider, within the bound.
No kernel may reach another device: no remote copies, remote signals or barrier semaphores. Data moves between devices by JAX's collectives and lax.ppermute only.
A program may use at most 64 MiB of HBM per device.

v0:
```python
import math
import jax
import jax.numpy as jnp
from jax import lax
from jax.sharding import PartitionSpec as P

TOPK = 8
CAP = 32
EPSILON = 1e-06


def from_behind(array, axis, by):
    size = lax.axis_size(axis)
    return lax.ppermute(array, axis, [(i, (i + by) % size) for i in range(size)])


def normalize(values):
    widened = values.astype(jnp.float32)
    factor = lax.rsqrt(jnp.mean(widened * widened, axis=-1, keepdims=True) + EPSILON)
    return (widened * factor, factor)


def slot_table(listed, window):
    hit_table = (listed[:, :, None] == jnp.arange(window, dtype=jnp.int32)[None, None, :]).astype(
        jnp.int32
    )
    flat_hits = hit_table.reshape(-1, window)
    before = jnp.cumsum(flat_hits, axis=0) - flat_hits
    ranked = jnp.sum(before * flat_hits, axis=1).reshape(listed.shape)
    return jnp.where(listed < window, listed * CAP + ranked, window * CAP)


def slot_owner(slot_ids, window):
    token_total = slot_ids.shape[0]
    token_index = jnp.repeat(jnp.arange(token_total, dtype=jnp.int32), slot_ids.shape[1])
    owners = (
        jnp.full((window * CAP + 1,), token_total, jnp.int32)
        .at[slot_ids.reshape(-1)]
        .set(token_index)
    )
    return owners[: window * CAP]


def slot_gates(slot_ids, gate_vals, window):
    filled = (
        jnp.zeros((window * CAP + 1,), jnp.float32)
        .at[slot_ids.reshape(-1)]
        .set(gate_vals.reshape(-1))
    )
    return filled[: window * CAP]


def pad_rows(row_table):
    extra = jnp.zeros((1, row_table.shape[-1]), row_table.dtype)
    return jnp.concatenate([row_table, extra], axis=0)


def local(
    section_input,
    saved_input,
    cotangent,
    routes_forward,
    gates_forward,
    routes_backward,
    gates_backward,
    gate_weight,
    up_weight,
    down_weight,
):
    window = lax.axis_size("expert")
    token_count = section_input.shape[1]
    model_width = section_input.shape[2]
    hidden_width = gate_weight.shape[3]
    gathered = (
        lax.all_gather(gate_weight, "dp", axis=2, tiled=True),
        lax.all_gather(up_weight, "dp", axis=2, tiled=True),
        lax.all_gather(down_weight, "dp", axis=2, tiled=True),
    )
    gate_full = gathered[0][0, 0]
    up_full = gathered[1][0, 0]
    down_full = gathered[2][0, 0]
    contract = (((1,), (1,)), ((), ()))
    normed, _ = normalize(section_input[0])
    slot_ids = slot_table(routes_forward[0], window)
    owners = slot_owner(slot_ids, window)
    sent_forward = pad_rows(normed.astype(jnp.bfloat16))[owners].reshape(window, CAP, model_width)
    saved_float, saved_scale = normalize(saved_input[0])
    back_slots = slot_table(routes_backward[0], window)
    back_owners = slot_owner(back_slots, window)
    back_gates = slot_gates(back_slots, gates_backward[0], window)
    sent_backward = pad_rows(saved_float.astype(jnp.bfloat16))[back_owners].reshape(
        window, CAP, model_width
    )
    grad_sent = (
        back_gates[:, None] * pad_rows(cotangent[0])[back_owners].astype(jnp.float32)
    ).astype(jnp.bfloat16)
    grad_sent = grad_sent.reshape(window, CAP, model_width)
    received = lax.all_to_all(sent_forward, "expert", split_axis=0, concat_axis=0, tiled=True)
    flat_rows = received.reshape(-1, model_width)
    gate_act = jnp.dot(flat_rows, gate_full, preferred_element_type=jnp.float32)
    up_act = jnp.dot(flat_rows, up_full, preferred_element_type=jnp.float32)
    hidden = (gate_act * jax.nn.sigmoid(gate_act) * up_act).astype(jnp.bfloat16)
    produced = jnp.dot(hidden, down_full, preferred_element_type=jnp.float32).astype(jnp.bfloat16)
    returned = lax.all_to_all(
        produced.reshape(received.shape), "expert", split_axis=0, concat_axis=0, tiled=True
    )
    received = (
        lax.all_to_all(sent_backward, "expert", split_axis=0, concat_axis=0, tiled=True),
        lax.all_to_all(grad_sent, "expert", split_axis=0, concat_axis=0, tiled=True),
    )
    received_rows = received[0]
    lead = received_rows.shape[:2]
    flat_rows = received_rows.reshape(-1, model_width)
    flat_grads = received[1].reshape(-1, model_width)
    gate_act = jnp.dot(flat_rows, gate_full, preferred_element_type=jnp.float32)
    up_act = jnp.dot(flat_rows, up_full, preferred_element_type=jnp.float32)
    sigma = jax.nn.sigmoid(gate_act)
    activated = gate_act * sigma
    hidden = (activated * up_act).astype(jnp.bfloat16)
    grad_hidden = lax.dot_general(
        flat_grads, down_full, contract, preferred_element_type=jnp.float32
    )
    grad_gate = (grad_hidden * up_act * sigma * (1.0 + gate_act * (1.0 - sigma))).astype(
        jnp.bfloat16
    )
    grad_up = (grad_hidden * activated).astype(jnp.bfloat16)
    grad_input = lax.dot_general(grad_gate, gate_full, contract, preferred_element_type=jnp.float32)
    grad_input = grad_input + lax.dot_general(
        grad_up, up_full, contract, preferred_element_type=jnp.float32
    )
    hidden, grad_gate, grad_up, grad_input = (
        hidden.reshape(lead + (hidden_width,)),
        grad_gate.reshape(lead + (hidden_width,)),
        grad_up.reshape(lead + (hidden_width,)),
        grad_input.astype(jnp.bfloat16).reshape(lead + (model_width,)),
    )
    sent_home = lax.all_to_all(grad_input, "expert", split_axis=0, concat_axis=0, tiled=True)
    grad_returned, expert_rows, expert_grads, hidden, grad_gate, grad_up = (
        sent_home,
        received[0],
        received[1],
        hidden,
        grad_gate,
        grad_up,
    )
    returned_pad = pad_rows(returned.reshape(window * CAP, model_width))
    mixed_sum = section_input[0].astype(jnp.float32)
    for slot_pos in range(TOPK):
        mixed_sum = mixed_sum + gates_forward[0][:, slot_pos, None] * returned_pad[
            slot_ids[:, slot_pos]
        ].astype(jnp.float32)
    handed = from_behind(mixed_sum.astype(jnp.bfloat16)[None], "section", 1)
    grad_pad = pad_rows(grad_returned.reshape(window * CAP, model_width))
    token_grad = jnp.zeros((token_count, model_width), jnp.float32)
    for slot_pos in range(TOPK):
        token_grad = token_grad + grad_pad[back_slots[:, slot_pos]].astype(jnp.float32)
    mean_term = jnp.mean(saved_float * token_grad, axis=-1, keepdims=True)
    input_grad = cotangent[0].astype(jnp.float32) + saved_scale * (
        token_grad - saved_float * mean_term
    )
    grad_back = from_behind(input_grad.astype(jnp.bfloat16)[None], "section", -1)
    rows_flat = expert_rows.reshape(-1, model_width)
    grads_flat = expert_grads.reshape(-1, model_width)
    hidden_flat = hidden.reshape(-1, hidden_width)
    gate_up = jnp.concatenate(
        [grad_gate.reshape(-1, hidden_width), grad_up.reshape(-1, hidden_width)], axis=1
    )
    transposed = (((0,), (0,)), ((), ()))
    left_part = rows_flat
    summed_in = lax.psum_scatter(
        lax.dot_general(left_part, gate_up, transposed, preferred_element_type=jnp.float32).astype(
            jnp.bfloat16
        ),
        "dp",
        scatter_dimension=0,
        tiled=True,
    ).astype(jnp.float32)
    left_part = hidden_flat
    summed_out = lax.psum_scatter(
        lax.dot_general(
            left_part, grads_flat, transposed, preferred_element_type=jnp.float32
        ).astype(jnp.bfloat16),
        "dp",
        scatter_dimension=0,
        tiled=True,
    ).astype(jnp.float32)
    grad_scale = 1.0 / math.sqrt(lax.axis_size("dp") * token_count)
    grad_gate_out = (summed_in[:, :hidden_width] * grad_scale)[None, None]
    grad_up_out = (summed_in[:, hidden_width:] * grad_scale)[None, None]
    grad_down_out = (summed_out * grad_scale)[None, None]
    return (handed, grad_back, grad_gate_out, grad_up_out, grad_down_out)


def solution(mesh):
    return jax.shard_map(
        local,
        mesh=mesh,
        in_specs=(
            P("section", ("dp", "expert"), None),
            P("section", ("dp", "expert"), None),
            P("section", ("dp", "expert"), None),
            P("section", ("dp", "expert"), None),
            P("section", ("dp", "expert"), None),
            P("section", ("dp", "expert"), None),
            P("section", ("dp", "expert"), None),
            P("section", "expert", "dp", None),
            P("section", "expert", "dp", None),
            P("section", "expert", "dp", None),
        ),
        out_specs=(
            P("section", ("dp", "expert"), None),
            P("section", ("dp", "expert"), None),
            P("section", "expert", "dp", None),
            P("section", "expert", "dp", None),
            P("section", "expert", "dp", None),
        ),
        check_vma=False,
    )
```

profile of v0, /device:TPU:2, one launch (start us, length us, event | category | flops | bytes accessed | tf_op | source)
XLA Modules:
  0.0 379.8 jit_solution(1343728989343063745)
XLA Ops:
  12.7 2.3 reduce-window.16
  15.9 4.3 %scatter_custom_fusion.2 = s32[257]{0:T(512)S(1)} fusion(s32[1024]{0:T(1024)S(1)} %bitcast.187, s32[1024]{0:T(1024)S(1)} %reshape.855, s32[]{:T(128)} %constant.17.clone.1), kind=kCustom, calls=%fused_computation.181 | custom fusion | bytes 1032 | tf_op jit(solution)/shard_map/scatter | solution.py:39
  20.2 2.0 gather_fusion.10
  22.2 4.5 %all-to-all-start.3 = ((bf16[8,32,1024]{2,1,0:T(8,128)(2,1)}), bf16[8,32,1024]{2,1,0:T(8,128)(2,1)S(1)}, u32[]{:S(2)}, u32[]{:S(2)}) async-start(bf16[8,32,1024]{2,1,0:T(8,128)(2,1)} %bitcast.37), calls=%async_computation.3 | async-start | bytes 1048576 | tf_op jit(solution)/shard_map/all_to_all | solution.py:108
  26.9 2.3 reduce-window.14
  31.1 4.3 %scatter_custom_fusion.1 = f32[257]{0:T(512)S(1)} fusion(s32[1024]{0:T(1024)S(1)} %bitcast.188, f32[1024]{0:T(1024)S(1)} %reshape.847, f32[]{:T(128)} %constant.13.clone.1), kind=kCustom, calls=%fused_computation.179 | custom fusion | bytes 1032 | tf_op jit(solution)/shard_map/scatter | solution.py:48
  37.0 4.4 %all-to-all-start.2 = ((bf16[8,32,1024]{2,1,0:T(8,128)(2,1)}), bf16[8,32,1024]{2,1,0:T(8,128)(2,1)S(1)}, u32[]{:S(2)}, u32[]{:S(2)}) async-start(bf16[8,32,1024]{2,1,0:T(8,128)(2,1)} %fusion.2), calls=%async_computation.2 | async-start | bytes 1048576 | tf_op jit(solution)/shard_map/all_to_all | solution.py:109
  41.4 43.9 %all-gather.4.cloned.1.call-done = bf16[1,1,1024,512]{3,2,1,0:T(8,128)(2,1)} async-done(((bf16[1,1,64,512]{3,2,1,0:T(8,128)(2,1)}), bf16[1,1,1024,512]{3,2,1,0:T(8,128)(2,1)}) %all-gather.4.cloned.1.call-update) | async-done | bytes 1048592 | tf_op jit(solution)/shard_map/all_gather | solution.py:75
  85.3 1.7 fusion.13
  87.0 67.9 %all-gather.6.cloned.1.call-done = bf16[1,1,1024,512]{3,2,1,0:T(8,128)(2,1)} async-done(((bf16[1,1,64,512]{3,2,1,0:T(8,128)(2,1)}), bf16[1,1,1024,512]{3,2,1,0:T(8,128)(2,1)}) %all-gather.6.cloned.1.call-update) | async-done | bytes 1048592 | tf_op jit(solution)/shard_map/all_gather | solution.py:76
  154.9 1.7 fusion.7
  156.6 1.5 convolution_convert_fusion.1
  158.6 4.3 %scatter_custom_fusion = s32[257]{0:T(512)S(1)} fusion(s32[1024]{0:T(1024)S(1)} %bitcast.189, s32[1024]{0:T(1024)S(1)} %reshape.855, s32[]{:T(128)} %constant.17.clone.1), kind=kCustom, calls=%fused_computation.183 | custom fusion | bytes 1032 | tf_op jit(solution)/shard_map/scatter | solution.py:39
  163.2 61.5 %all-gather.8.cloned.1.call-done = bf16[1,1,512,1024]{3,2,1,0:T(8,128)(2,1)} async-done(((bf16[1,1,32,1024]{3,2,1,0:T(8,128)(2,1)}), bf16[1,1,512,1024]{3,2,1,0:T(8,128)(2,1)}) %all-gather.8.cloned.1.call-update) | async-done | bytes 1048592 | tf_op jit(solution)/shard_map/all_gather | solution.py:77
  224.7 1.9 multiply_convert_fusion.1
  226.7 2.1 convolution_convert_fusion
  228.8 2.0 gather_fusion
  230.8 4.4 %all-to-all-start = ((bf16[8,32,1024]{2,1,0:T(8,128)(2,1)}), bf16[8,32,1024]{2,1,0:T(8,128)(2,1)S(1)}, u32[]{:S(2)}, u32[]{:S(2)}) async-start(bf16[8,32,1024]{2,1,0:T(8,128)(2,1)} %bitcast.6), calls=%async_computation | async-start | bytes 1048576 | tf_op jit(solution)/shard_map/all_to_all | solution.py:98
  238.4 1.6 slice_bitcast_fusion.7
  240.0 5.5 %all-to-all-done = bf16[8,32,1024]{2,1,0:T(8,128)(2,1)S(1)} async-done(((bf16[8,32,1024]{2,1,0:T(8,128)(2,1)}), bf16[8,32,1024]{2,1,0:T(8,128)(2,1)S(1)}, u32[]{:S(2)}, u32[]{:S(2)}) %all-to-all-start) | async-done | bytes 524320 | tf_op jit(solution)/shard_map/all_to_all | solution.py:98
  245.5 1.2 fusion.15
  246.8 3.0 convolution_convert_fusion.2
  249.8 3.7 all-to-all-start.1
  253.9 1.3 fusion
  255.2 8.3 %all-to-all-done.1 = bf16[8,32,1024]{2,1,0:T(8,128)(2,1)S(1)} async-done(((bf16[8,32,1024]{2,1,0:T(8,128)(2,1)}), bf16[8,32,1024]{2,1,0:T(8,128)(2,1)S(1)}, u32[]{:S(2)}, u32[]{:S(2)}) %all-to-all-start.1) | async-done | bytes 524320 | tf_op jit(solution)/shard_map/all_to_all | solution.py:104
  263.5 3.5 all-to-all-start.4
  276.3 1.2 fusion.33
  277.5 3.4 collective-permute-start
  289.3 2.5 collective-permute-start.1
  291.8 7.7 %collective-permute-done.1 = bf16[1,128,1024]{2,1,0:T(8,128)(2,1)S(1)} collective-permute-done((bf16[1,128,1024]{2,1,0:T(8,128)(2,1)S(1)}, bf16[1,128,1024]{2,1,0:T(8,128)(2,1)S(1)}, u32[]{:S(2)}, u32[]{:S(2)}) %collective-permute-start.1) | collective-permute-done | bytes 262176 | tf_op jit(solution)/shard_map/ppermute | solution.py:14
  299.5 1.5 multiply_bitcast_fusion
  301.0 69.2 %reduce-scatter.3.cloned.1.call-done = bf16[64,1024]{1,0:T(8,128)(2,1)} async-done(((bf16[1024,1024]{1,0:T(8,128)(2,1)}), bf16[64,1024]{1,0:T(8,128)(2,1)}) %reduce-scatter.3.cloned.1.call-update) | async-done | bytes 131088 | tf_op jit(solution)/shard_map/reduce_scatter | solution.py:170
  (138 shorter events, 34.9 us)
Async XLA Ops:
  7.2 78.2 %all-gather.4.cloned.1.call-start = ((), (), s32[]{:S(2)}) async-start(), calls=%async_computation.7 | async-start | bytes 1114112 | tf_op jit(solution)/shard_map/all_gather | solution.py:75
  7.9 147.0 %all-gather.6.cloned.1.call-start = ((), (), s32[]{:S(2)}) async-start(), calls=%async_computation.8 | async-start | bytes 1114112 | tf_op jit(solution)/shard_map/all_gather | solution.py:76
  8.6 216.1 %all-gather.8.cloned.1.call-start = ((), (), s32[]{:S(2)}) async-start(), calls=%async_computation.9 | async-start | bytes 1114112 | tf_op jit(solution)/shard_map/all_gather | solution.py:77
  11.6 3.9 %copy-start.7 = (f32[128]{0:T(128)}, f32[128]{0:T(128)S(1)}, u32[]{:S(2)}) copy-start(f32[128]{0:T(128)S(1)} %add_rsqrt_fusion) | copy-start | bytes 1540
  20.2 6.5 %copy-start.9 = (s32[1,128,8]{1,2,0:T(8,128)S(1)}, s32[1,128,8]{1,2,0:T(8,128)}, u32[]{:S(2)}) copy-start(s32[1,128,8]{1,2,0:T(8,128)} %param.13) | copy-start | bytes 12292
  20.2 9.5 %copy-start.4 = (bf16[1,128,1024]{2,1,0:T(8,128)(2,1)S(1)}, bf16[1,128,1024]{2,1,0:T(8,128)(2,1)}, u32[]{:S(2)}) copy-start(bf16[1,128,1024]{2,1,0:T(8,128)(2,1)} %param.12) | copy-start | bytes 786436
  22.2 14.8 %all-to-all-start.3 = ((bf16[8,32,1024]{2,1,0:T(8,128)(2,1)}), bf16[8,32,1024]{2,1,0:T(8,128)(2,1)S(1)}, u32[]{:S(2)}, u32[]{:S(2)}) async-start(bf16[8,32,1024]{2,1,0:T(8,128)(2,1)} %bitcast.37), calls=%async_computation.3 | async-start | bytes 1048576 | tf_op jit(solution)/shard_map/all_to_all | solution.py:108
  29.7 1.2 copy-start.10
  37.0 119.6 %all-to-all-start.2 = ((bf16[8,32,1024]{2,1,0:T(8,128)(2,1)}), bf16[8,32,1024]{2,1,0:T(8,128)(2,1)S(1)}, u32[]{:S(2)}, u32[]{:S(2)}) async-start(bf16[8,32,1024]{2,1,0:T(8,128)(2,1)} %fusion.2), calls=%async_computation.2 | async-start | bytes 1048576 | tf_op jit(solution)/shard_map/all_to_all | solution.py:109
  41.3 258.2 %reduce-scatter.5.cloned.1.call-start = ((), (), s32[]{:S(2)}) async-start(), calls=%async_computation.11 | async-start | bytes 1114112 | tf_op jit(solution)/shard_map/reduce_scatter | solution.py:179
  156.6 6.5 %copy-start.6 = (f32[256,512]{1,0:T(8,128)}, f32[256,512]{1,0:T(8,128)S(1)}, u32[]{:S(2)}) copy-start(f32[256,512]{1,0:T(8,128)S(1)} %fusion.7) | copy-start | bytes 1572868
  156.6 6.3 %copy-start.3 = (bf16[1,128,1024]{2,1,0:T(8,128)(2,1)S(1)}, bf16[1,128,1024]{2,1,0:T(8,128)(2,1)}, u32[]{:S(2)}) copy-start(bf16[1,128,1024]{2,1,0:T(8,128)(2,1)} %param.10) | copy-start | bytes 786436
  158.1 212.0 %reduce-scatter.3.cloned.1.call-start = ((), (), s32[]{:S(2)}) async-start(), calls=%async_computation.10 | async-start | bytes 2228224 | tf_op jit(solution)/shard_map/reduce_scatter | solution.py:170
  230.8 14.7 %copy-start = (bf16[1,1,1024,512]{3,2,1,0:T(8,128)(2,1)S(1)}, bf16[1,1,1024,512]{3,2,1,0:T(8,128)(2,1)}, u32[]{:S(2)}) copy-start(bf16[1,1,1024,512]{3,2,1,0:T(8,128)(2,1)} %all-gather.4.cloned.1.call-done) | copy-start | bytes 3145732
  230.8 16.0 %copy-start.1 = (bf16[1,1,1024,512]{3,2,1,0:T(8,128)(2,1)S(1)}, bf16[1,1,1024,512]{3,2,1,0:T(8,128)(2,1)}, u32[]{:S(2)}) copy-start(bf16[1,1,1024,512]{3,2,1,0:T(8,128)(2,1)} %all-gather.6.cloned.1.call-done) | copy-start | bytes 3145732
  230.8 14.7 %all-to-all-start = ((bf16[8,32,1024]{2,1,0:T(8,128)(2,1)}), bf16[8,32,1024]{2,1,0:T(8,128)(2,1)S(1)}, u32[]{:S(2)}, u32[]{:S(2)}) async-start(bf16[8,32,1024]{2,1,0:T(8,128)(2,1)} %bitcast.6), calls=%async_computation | async-start | bytes 1048576 | tf_op jit(solution)/shard_map/all_to_all | solution.py:98
  249.8 13.7 %all-to-all-start.1 = ((bf16[8,32,1024]{2,1,0:T(8,128)(2,1)}), bf16[8,32,1024]{2,1,0:T(8,128)(2,1)S(1)}, u32[]{:S(2)}, u32[]{:S(2)}) async-start(bf16[8,32,1024]{2,1,0:T(8,128)(2,1)} %bitcast.181), calls=%async_computation.1 | async-start | bytes 1048576 | tf_op jit(solution)/shard_map/all_to_all | solution.py:104
  263.5 17.4 %all-to-all-start.4 = ((bf16[8,32,1024]{2,1,0:T(8,128)(2,1)}), bf16[8,32,1024]{2,1,0:T(8,128)(2,1)S(1)}, u32[]{:S(2)}, u32[]{:S(2)}) async-start(bf16[8,32,1024]{2,1,0:T(8,128)(2,1)} %bitcast.39), calls=%async_computation.4 | async-start | bytes 1048576 | tf_op jit(solution)/shard_map/all_to_all | solution.py:137
  274.2 2.0 copy-start.11
  274.2 2.0 copy-start.12
  274.2 2.0 copy-start.13
  274.2 2.0 copy-start.14
  274.2 2.0 copy-start.15
  274.2 2.0 copy-start.16
  274.2 2.0 copy-start.17
  274.2 2.0 copy-start.18
  277.5 14.3 %collective-permute-start = (bf16[1,128,1024]{2,1,0:T(8,128)(2,1)}, bf16[1,128,1024]{2,1,0:T(8,128)(2,1)S(1)}, u32[]{:S(2)}, u32[]{:S(2)}) collective-permute-start(bf16[1,128,1024]{2,1,0:T(8,128)(2,1)} %fusion.33), channel_id=1, source_target_pairs={{0,128},{128,256},{256,384},{384,0},{1,129},{129,257},{257,385},{3... | collective-permute-start | bytes 786440 | tf_op jit(solution)/shard_map/ppermute | solution.py:14
  286.3 2.3 copy-start.2
  286.3 2.3 copy-start.8
  287.5 1.6 copy-start.5
  289.3 10.2 %collective-permute-start.1 = (bf16[1,128,1024]{2,1,0:T(8,128)(2,1)S(1)}, bf16[1,128,1024]{2,1,0:T(8,128)(2,1)S(1)}, u32[]{:S(2)}, u32[]{:S(2)}) collective-permute-start(bf16[1,128,1024]{2,1,0:T(8,128)(2,1)S(1)} %fusion.39), channel_id=1, source_target_pairs={{0,384},{128,0},{256,128},{384,256},{1,385},{129,1},{257,129},{385... | collective-permute-start | bytes 786440 | tf_op jit(solution)/shard_map/ppermute | solution.py:14
Sparse Core Ops, SparseCore 0:
  10.1 75.2 all-gather.3
  87.4 67.4 all-gather.5
  157.0 67.6 all-gather.7
  227.4 68.3 reduce-scatter.4
  298.5 71.6 reduce-scatter.2
where the time goes:
time: 381 us; the launch traced here: 380 us
  waiting for transfers between devices  267 us (70%)
  local copies, waits for them, and re-layouts  39.5 us (10%)
  starting transfers between devices  26.4 us (7%)
  other arithmetic  17.9 us (5%)
  matrix products  14.8 us (4%)
  between operations  14.4 us (4%)
    reduce_scatter x1, waiting for transfers between devices, local(): lax.psum_scatter(lax.dot_general(left_part, gate_up, transposed, preferre...  69.2 us
    all_gather x1, waiting for transfers between devices, local(): lax.all_gather(up_weight, 'dp', axis=2, tiled=True)  67.9 us
    all_gather x1, waiting for transfers between devices, local(): lax.all_gather(down_weight, 'dp', axis=2, tiled=True)  61.5 us
    all_gather x1, waiting for transfers between devices, local(): lax.all_gather(gate_weight, 'dp', axis=2, tiled=True)  43.9 us
    scatter x2, local copies, waits for them, and re-layouts, slot_owner(): owners = jnp.full((window * CAP + 1,), token_total, jnp.int32).at[slot_id...  8.61 us
    all_to_all x1, waiting for transfers between devices, local(): lax.all_to_all(produced.reshape(received.shape), 'expert', split_axis=0,...  8.33 us
    gather x8, local copies, waits for them, and re-layouts, local(): returned_pad[slot_ids[:, slot_pos]].astype(jnp.float32)  7.86 us
    ppermute x2, waiting for transfers between devices, from_behind(): lax.ppermute(array, axis, [(i, (i + by) % size) for i in range(size)])  7.75 us
  transfers between devices with their start and end apart: 12, of which 8 were waited for; matrix products, arithmetic and copies ran while one was open for 18% of the time, Pallas kernels for 0%

commit v1 on v0

--- a/solution.py
+++ b/solution.py
@@ -73,7 +73,9 @@
     hidden_width = gate_weight.shape[3]
     gathered = (
         lax.all_gather(gate_weight, "dp", axis=2, tiled=True),
-        lax.all_gather(up_weight, "dp", axis=2, tiled=True),
+        jnp.concatenate(
+            lax.all_to_all(jnp.stack([up_weight] * lax.axis_size("dp")), "dp", 0, 0), axis=2
+        ),
         lax.all_gather(down_weight, "dp", axis=2, tiled=True),
     )
     gate_full = gathered[0][0, 0]

time: 381 us -> 361 us (0.948)
  waiting for transfers between devices: 267 us -> 228 us
  blocking collectives: 0 us -> 14.6 us
  starting transfers between devices: 26.4 us -> 36.3 us
    all_gather x1 -> x0, waiting for transfers between devices: 67.9 us -> none  [local(): lax.all_gather(up_weight, 'dp', axis=2, tiled=True)]
    all_to_all x1, waiting for transfers between devices: 0.43 us -> 41.5 us  [local(): lax.all_to_all(jnp.stack([up_weight] * lax.axis_size('dp')), 'dp', 0, 0)]
    all_gather x1, waiting for transfers between devices: 43.9 us -> 28.5 us  [local(): lax.all_gather(gate_weight, 'dp', axis=2, tiled=True)]
    all_to_all x0 -> x1, blocking collectives: none -> 14.6 us  [local(): lax.all_to_all(sent_backward, 'expert', split_axis=0, concat_axis=0, tile...]
    all_to_all x1, starting transfers between devices: 4.47 us -> 15.2 us  [local(): lax.all_to_all(jnp.stack([up_weight] * lax.axis_size('dp')), 'dp', 0, 0)]
    all_to_all x1, waiting for transfers between devices: 5.54 us -> 9.47 us  [local(): lax.all_to_all(sent_forward, 'expert', split_axis=0, concat_axis=0, tiled...]
  transfers between devices with their start and end apart: 12 -> 11, of which waited for: 8 -> 7; matrix products, arithmetic and copies ran while one was open for 18% -> 14% of each run, Pallas kernels for 0% -> 0%
where the time goes in v1:
time: 361 us; the launch traced here: 360 us
  waiting for transfers between devices  228 us (63%)
  local copies, waits for them, and re-layouts  36.4 us (10%)
  starting transfers between devices  36.3 us (10%)
  matrix products  15.7 us (4%)
  blocking collectives  14.6 us (4%)
  other arithmetic  14.4 us (4%)
  between operations  14.3 us (4%)
    reduce_scatter x1, waiting for transfers between devices, local(): lax.psum_scatter(lax.dot_general(left_part, gate_up, transposed, preferre...  72.1 us
    all_gather x1, waiting for transfers between devices, local(): lax.all_gather(down_weight, 'dp', axis=2, tiled=True)  59.1 us
    all_to_all x1, waiting for transfers between devices, local(): lax.all_to_all(jnp.stack([up_weight] * lax.axis_size('dp')), 'dp', 0, 0)  41.5 us
    all_gather x1, waiting for transfers between devices, local(): lax.all_gather(gate_weight, 'dp', axis=2, tiled=True)  28.5 us
    all_to_all x1, starting transfers between devices, local(): lax.all_to_all(jnp.stack([up_weight] * lax.axis_size('dp')), 'dp', 0, 0)  15.2 us
    all_to_all x1, blocking collectives, local(): lax.all_to_all(sent_backward, 'expert', split_axis=0, concat_axis=0, tile...  14.6 us
    all_to_all x1, waiting for transfers between devices, local(): lax.all_to_all(sent_forward, 'expert', split_axis=0, concat_axis=0, tiled...  9.47 us
    scatter x2, local copies, waits for them, and re-layouts, slot_owner(): owners = jnp.full((window * CAP + 1,), token_total, jnp.int32).at[slot_id...  8.61 us
  transfers between devices with their start and end apart: 11, of which 7 were waited for; matrix products, arithmetic and copies ran while one was open for 14% of the time, Pallas kernels for 0%

profile of v1, /device:TPU:2, one launch (start us, length us, event | category | flops | bytes accessed | tf_op | source)
XLA Modules:
  0.0 359.9 jit_solution(8022468386849708122)
XLA Ops:
  10.4 2.3 reduce-window.16
  13.6 4.3 %scatter_custom_fusion.2 = s32[257]{0:T(512)S(1)} fusion(s32[1024]{0:T(1024)S(1)} %bitcast.189, s32[1024]{0:T(1024)S(1)} %reshape.858, s32[]{:T(128)} %constant.17.clone.1), kind=kCustom, calls=%fused_computation.177 | custom fusion | bytes 1032 | tf_op jit(solution)/shard_map/scatter | solution.py:39
  19.2 14.6 %all_to_all.30 = bf16[8,32,1024]{2,1,0:T(8,128)(2,1)S(1)} all-to-all(bf16[8,32,1024]{2,1,0:T(8,128)(2,1)S(1)} %bitcast.174), channel_id=1, replica_groups=mesh['section'=4,'dp'=16,'expert'=8] {'expert'}, dimensions={0} | all-to-all | bytes 1048576 | tf_op jit(solution)/shard_map/all_to_all | solution.py:110
  34.9 15.2 %all-to-all-start.1 = ((bf16[16,1,1,64,512]{4,3,2,1,0:T(8,128)(2,1)}), bf16[16,1,1,64,512]{4,3,2,1,0:T(8,128)(2,1)S(1)}, u32[]{:S(2)}, u32[]{:S(2)}) async-start(bf16[16,1,1,64,512]{4,3,2,1,0:T(8,128)(2,1)} %stack.2), calls=%async_computation.1 | async-start | bytes 2097152 | tf_op jit(solution)/shard_map/all_to_all | solution.py:77
  51.9 2.3 reduce-window.14
  54.6 1.2 gather_fusion.9
  56.0 4.3 %scatter_custom_fusion.1 = f32[257]{0:T(512)S(1)} fusion(s32[1024]{0:T(1024)S(1)} %bitcast.190, f32[1024]{0:T(1024)S(1)} %reshape.850, f32[]{:T(128)} %constant.13.clone.1), kind=kCustom, calls=%fused_computation.175 | custom fusion | bytes 1032 | tf_op jit(solution)/shard_map/scatter | solution.py:48
  61.5 41.5 %all-to-all-done.1 = bf16[16,1,1,64,512]{4,3,2,1,0:T(8,128)(2,1)S(1)} async-done(((bf16[16,1,1,64,512]{4,3,2,1,0:T(8,128)(2,1)}), bf16[16,1,1,64,512]{4,3,2,1,0:T(8,128)(2,1)S(1)}, u32[]{:S(2)}, u32[]{:S(2)}) %all-to-all-start.1) | async-done | bytes 1048608 | tf_op jit(solution)/shard_map/all_to_all | solution.py:77
  102.9 3.5 all-to-all-start.3
  106.5 28.5 %all-gather.3.cloned.1.call-done = bf16[1,1,1024,512]{3,2,1,0:T(8,128)(2,1)} async-done(((bf16[1,1,64,512]{3,2,1,0:T(8,128)(2,1)}), bf16[1,1,1024,512]{3,2,1,0:T(8,128)(2,1)}) %all-gather.3.cloned.1.call-update) | async-done | bytes 1048592 | tf_op jit(solution)/shard_map/all_gather | solution.py:75
  135.0 1.7 fusion.8
  136.6 1.2 fusion.83
  137.9 2.6 convolution_convert_fusion.1
  140.9 4.3 %scatter_custom_fusion = s32[257]{0:T(512)S(1)} fusion(s32[1024]{0:T(1024)S(1)} %bitcast.191, s32[1024]{0:T(1024)S(1)} %reshape.858, s32[]{:T(128)} %constant.17.clone.1), kind=kCustom, calls=%fused_computation.179 | custom fusion | bytes 1032 | tf_op jit(solution)/shard_map/scatter | solution.py:39
  145.5 59.1 %all-gather.5.cloned.1.call-done = bf16[1,1,512,1024]{3,2,1,0:T(8,128)(2,1)} async-done(((bf16[1,1,32,1024]{3,2,1,0:T(8,128)(2,1)}), bf16[1,1,512,1024]{3,2,1,0:T(8,128)(2,1)}) %all-gather.5.cloned.1.call-update) | async-done | bytes 1048592 | tf_op jit(solution)/shard_map/all_gather | solution.py:79
  204.6 2.1 multiply_convert_fusion.1
  206.7 2.1 convolution_convert_fusion
  208.8 2.0 gather_fusion
  210.8 4.4 %all-to-all-start = ((bf16[8,32,1024]{2,1,0:T(8,128)(2,1)}), bf16[8,32,1024]{2,1,0:T(8,128)(2,1)S(1)}, u32[]{:S(2)}, u32[]{:S(2)}) async-start(bf16[8,32,1024]{2,1,0:T(8,128)(2,1)} %bitcast.6), calls=%async_computation | async-start | bytes 1048576 | tf_op jit(solution)/shard_map/all_to_all | solution.py:100
  216.1 9.5 %all-to-all-done = bf16[8,32,1024]{2,1,0:T(8,128)(2,1)S(1)} async-done(((bf16[8,32,1024]{2,1,0:T(8,128)(2,1)}), bf16[8,32,1024]{2,1,0:T(8,128)(2,1)S(1)}, u32[]{:S(2)}, u32[]{:S(2)}) %all-to-all-start) | async-done | bytes 524320 | tf_op jit(solution)/shard_map/all_to_all | solution.py:100
  225.6 1.3 fusion.10
  226.8 3.0 convolution_convert_fusion.2
  229.8 3.7 %all-to-all-start.2 = ((bf16[8,32,1024]{2,1,0:T(8,128)(2,1)}), bf16[8,32,1024]{2,1,0:T(8,128)(2,1)S(1)}, u32[]{:S(2)}, u32[]{:S(2)}) async-start(bf16[8,32,1024]{2,1,0:T(8,128)(2,1)} %bitcast.182), calls=%async_computation.2 | async-start | bytes 1048576 | tf_op jit(solution)/shard_map/all_to_all | solution.py:106
  234.0 1.3 fusion
  235.2 8.5 %all-to-all-done.2 = bf16[8,32,1024]{2,1,0:T(8,128)(2,1)S(1)} async-done(((bf16[8,32,1024]{2,1,0:T(8,128)(2,1)}), bf16[8,32,1024]{2,1,0:T(8,128)(2,1)S(1)}, u32[]{:S(2)}, u32[]{:S(2)}) %all-to-all-start.2) | async-done | bytes 524320 | tf_op jit(solution)/shard_map/all_to_all | solution.py:106
  243.7 3.5 all-to-all-start.5
  254.2 1.2 fusion.28
  255.4 3.4 collective-permute-start
  266.4 2.5 collective-permute-start.1
  268.9 7.7 %collective-permute-done.1 = bf16[1,128,1024]{2,1,0:T(8,128)(2,1)S(1)} collective-permute-done((bf16[1,128,1024]{2,1,0:T(8,128)(2,1)S(1)}, bf16[1,128,1024]{2,1,0:T(8,128)(2,1)S(1)}, u32[]{:S(2)}, u32[]{:S(2)}) %collective-permute-start.1) | collective-permute-done | bytes 262176 | tf_op jit(solution)/shard_map/ppermute | solution.py:14
  276.6 1.5 multiply_bitcast_fusion
  278.2 72.1 %reduce-scatter.3.cloned.1.call-done = bf16[64,1024]{1,0:T(8,128)(2,1)} async-done(((bf16[1024,1024]{1,0:T(8,128)(2,1)}), bf16[64,1024]{1,0:T(8,128)(2,1)}) %reduce-scatter.3.cloned.1.call-update) | async-done | bytes 131088 | tf_op jit(solution)/shard_map/reduce_scatter | solution.py:172
  (119 shorter events, 29.5 us)
Async XLA Ops:
  18.0 15.8 %copy-start.6 = (bf16[1,1,64,512]{3,2,1,0:T(8,128)(2,1)S(1)}, bf16[1,1,64,512]{3,2,1,0:T(8,128)(2,1)}, u32[]{:S(2)}) copy-start(bf16[1,1,64,512]{3,2,1,0:T(8,128)(2,1)} %param.18) | copy-start | bytes 196612
  19.2 32.4 %copy-start.7 = (s32[1,128,8]{1,2,0:T(8,128)S(1)}, s32[1,128,8]{1,2,0:T(8,128)}, u32[]{:S(2)}) copy-start(s32[1,128,8]{1,2,0:T(8,128)} %param.13) | copy-start | bytes 12292
  33.8 20.8 %copy-start.3 = (bf16[1,128,1024]{2,1,0:T(8,128)(2,1)S(1)}, bf16[1,128,1024]{2,1,0:T(8,128)(2,1)}, u32[]{:S(2)}) copy-start(bf16[1,128,1024]{2,1,0:T(8,128)(2,1)} %param.12) | copy-start | bytes 786436
  34.9 68.1 %all-to-all-start.1 = ((bf16[16,1,1,64,512]{4,3,2,1,0:T(8,128)(2,1)}), bf16[16,1,1,64,512]{4,3,2,1,0:T(8,128)(2,1)S(1)}, u32[]{:S(2)}, u32[]{:S(2)}) async-start(bf16[16,1,1,64,512]{4,3,2,1,0:T(8,128)(2,1)} %stack.2), calls=%async_computation.1 | async-start | bytes 2097152 | tf_op jit(solution)/shard_map/all_to_all | solution.py:77
  50.1 84.9 %all-gather.3.cloned.1.call-start = ((), (), s32[]{:S(2)}) async-start(), calls=%async_computation.8 | async-start | bytes 1114112 | tf_op jit(solution)/shard_map/all_gather | solution.py:75
  50.8 153.8 %all-gather.5.cloned.1.call-start = ((), (), s32[]{:S(2)}) async-start(), calls=%async_computation.9 | async-start | bytes 1114112 | tf_op jit(solution)/shard_map/all_gather | solution.py:79
  54.6 1.2 copy-start.8
  102.9 35.0 %all-to-all-start.3 = ((bf16[8,32,1024]{2,1,0:T(8,128)(2,1)}), bf16[8,32,1024]{2,1,0:T(8,128)(2,1)S(1)}, u32[]{:S(2)}, u32[]{:S(2)}) async-start(bf16[8,32,1024]{2,1,0:T(8,128)(2,1)} %fusion.2), calls=%async_computation.3 | async-start | bytes 1048576 | tf_op jit(solution)/shard_map/all_to_all | solution.py:111
  106.4 170.2 %reduce-scatter.5.cloned.1.call-start = ((), (), s32[]{:S(2)}) async-start(), calls=%async_computation.11 | async-start | bytes 1114112 | tf_op jit(solution)/shard_map/reduce_scatter | solution.py:181
  136.6 3.9 %copy-start.5 = (f32[256,512]{1,0:T(8,128)}, f32[256,512]{1,0:T(8,128)S(1)}, u32[]{:S(2)}) copy-start(f32[256,512]{1,0:T(8,128)S(1)} %fusion.8) | copy-start | bytes 1572868
  137.9 7.4 %copy-start.2 = (bf16[1,128,1024]{2,1,0:T(8,128)(2,1)S(1)}, bf16[1,128,1024]{2,1,0:T(8,128)(2,1)}, u32[]{:S(2)}) copy-start(bf16[1,128,1024]{2,1,0:T(8,128)(2,1)} %param.10) | copy-start | bytes 786436
  140.5 209.8 %reduce-scatter.3.cloned.1.call-start = ((), (), s32[]{:S(2)}) async-start(), calls=%async_computation.10 | async-start | bytes 2228224 | tf_op jit(solution)/shard_map/reduce_scatter | solution.py:172
  210.8 5.2 %copy-start.9 = (f32[1,128,8]{1,2,0:T(8,128)S(1)}, f32[1,128,8]{1,2,0:T(8,128)}, u32[]{:S(2)}) copy-start(f32[1,128,8]{1,2,0:T(8,128)} %param.14) | copy-start | bytes 12292
  210.8 14.7 %copy-start = (bf16[1,1,1024,512]{3,2,1,0:T(8,128)(2,1)S(1)}, bf16[1,1,1024,512]{3,2,1,0:T(8,128)(2,1)}, u32[]{:S(2)}) copy-start(bf16[1,1,1024,512]{3,2,1,0:T(8,128)(2,1)} %all-gather.3.cloned.1.call-done) | copy-start | bytes 3145732
  210.8 14.7 %all-to-all-start = ((bf16[8,32,1024]{2,1,0:T(8,128)(2,1)}), bf16[8,32,1024]{2,1,0:T(8,128)(2,1)S(1)}, u32[]{:S(2)}, u32[]{:S(2)}) async-start(bf16[8,32,1024]{2,1,0:T(8,128)(2,1)} %bitcast.6), calls=%async_computation | async-start | bytes 1048576 | tf_op jit(solution)/shard_map/all_to_all | solution.py:100
  229.8 13.9 %all-to-all-start.2 = ((bf16[8,32,1024]{2,1,0:T(8,128)(2,1)}), bf16[8,32,1024]{2,1,0:T(8,128)(2,1)S(1)}, u32[]{:S(2)}, u32[]{:S(2)}) async-start(bf16[8,32,1024]{2,1,0:T(8,128)(2,1)} %bitcast.182), calls=%async_computation.2 | async-start | bytes 1048576 | tf_op jit(solution)/shard_map/all_to_all | solution.py:106
  243.7 15.0 %all-to-all-start.5 = ((bf16[8,32,1024]{2,1,0:T(8,128)(2,1)}), bf16[8,32,1024]{2,1,0:T(8,128)(2,1)S(1)}, u32[]{:S(2)}, u32[]{:S(2)}) async-start(bf16[8,32,1024]{2,1,0:T(8,128)(2,1)} %bitcast.40), calls=%async_computation.5 | async-start | bytes 1048576 | tf_op jit(solution)/shard_map/all_to_all | solution.py:139
  255.4 13.5 %collective-permute-start = (bf16[1,128,1024]{2,1,0:T(8,128)(2,1)}, bf16[1,128,1024]{2,1,0:T(8,128)(2,1)S(1)}, u32[]{:S(2)}, u32[]{:S(2)}) collective-permute-start(bf16[1,128,1024]{2,1,0:T(8,128)(2,1)} %fusion.28), channel_id=1, source_target_pairs={{0,128},{128,256},{256,384},{384,0},{1,129},{129,257},{257,385},{3... | collective-permute-start | bytes 786440 | tf_op jit(solution)/shard_map/ppermute | solution.py:14
  264.0 1.7 copy-start.1
  264.9 1.3 copy-start.4
  266.4 10.2 %collective-permute-start.1 = (bf16[1,128,1024]{2,1,0:T(8,128)(2,1)S(1)}, bf16[1,128,1024]{2,1,0:T(8,128)(2,1)S(1)}, u32[]{:S(2)}, u32[]{:S(2)}) collective-permute-start(bf16[1,128,1024]{2,1,0:T(8,128)(2,1)S(1)} %fusion.34), channel_id=1, source_target_pairs={{0,384},{128,0},{256,128},{384,256},{1,385},{129,1},{257,129},{385... | collective-permute-start | bytes 786440 | tf_op jit(solution)/shard_map/ppermute | solution.py:14
Sparse Core Ops, SparseCore 0:
  53.0 81.9 all-gather.2
  137.1 67.4 all-gather.4
  207.4 68.3 reduce-scatter.4
  278.5 71.7 reduce-scatter.2
